TPU v7x, 32 devices: a whole 2x2x4 slice. The times are simulated.
32 devices in a mesh: space: 8 (over z, y), chan: 2 (over core), filt: 2 (over x).
Axes of the slice: x: 2, y: 2, z: 4, core: 2. Of those that a mesh axis runs over, the one named last changes fastest.
Arguments:
- activation: bfloat16 [8, 512, 512], P('space', ('chan', 'filt')), may hold values from -6 to 6
- kernel: bfloat16 [3, 3, 3, 512, 512], P(None, None, None, 'filt', 'chan'), may hold values from -0.0546875 to 0.0546875
- out_grad: bfloat16 [8, 512, 512], P('space', 'filt', 'chan'), may hold values from -6 to 6
Outputs:
- output: bfloat16 [8, 512, 512], P('space', 'filt', 'chan')
- input_grad: bfloat16 [8, 512, 512], P('space', ('chan', 'filt'))
- kernel_grad: float32 [3, 3, 3, 512, 512], P(None, None, None, 'filt', 'chan')
All inputs are finite; a program needn't handle non-finite values.
Results may differ from a plain program's by a relative error of at most 0.001.
Values may be sent and summed in bfloat16 or wider, within the bound.
A program may use at most 128 MiB of HBM per device.

v0:
```python
import jax
import jax.numpy as jnp
from jax import lax
from jax.sharding import PartitionSpec as P

W = 16


def padded(x, sides, width):
    for axis, dim in sides:
        size, length = (lax.axis_size(axis), x.shape[dim])
        up = [(i, (i + 1) % size) for i in range(size - 1)]
        down = [(j, i) for i, j in up]
        last = lax.slice_in_dim(x, length - width, length, axis=dim)
        first = lax.slice_in_dim(x, 0, width, axis=dim)
        before = lax.ppermute(last, axis, up)
        after = lax.ppermute(first, axis, down)
        x = jnp.concatenate([before, x, after], axis=dim)
    return x


def plane_window(widened, plane, row_step, col_step, masks):
    begin = row_step * W + col_step
    return widened[:, :, begin : begin + plane] * masks[col_step]


def body(activation, kernel, out_grad):
    depth = activation.shape[0]
    plane = activation.shape[2]
    panels = lax.all_gather(activation, "filt", axis=1, tiled=True)
    rimmed = padded(panels, (("space", 0),), 1)
    grad_full = lax.all_gather(out_grad, "chan", axis=2, tiled=True)
    grad_rimmed = padded(grad_full, (("space", 0),), 1)
    column = lax.iota(jnp.int32, plane) % W
    masks = [
        ((column + step - 1 >= 0) & (column + step - 1 < W)).astype(jnp.bfloat16)
        for step in range(3)
    ]
    chan_local = rimmed.shape[1]
    filt_local = grad_rimmed.shape[1]
    wide_input = jnp.pad(rimmed, ((0, 0), (0, 0), (W + 1, W + 1)))
    wide_grad = jnp.pad(grad_rimmed, ((0, 0), (0, 0), (W + 1, W + 1)))
    forward = jnp.zeros((depth, filt_local, plane), jnp.float32)
    backward = jnp.zeros((depth, chan_local, plane), jnp.float32)
    taps = []
    for a in range(3):
        input_slab = wide_input[a : a + depth]
        grad_slab = wide_grad[2 - a : 2 - a + depth]
        for b in range(3):
            window = jnp.concatenate(
                [plane_window(input_slab, plane, b, c, masks) for c in range(3)], axis=1
            )
            grad_window = jnp.concatenate(
                [plane_window(grad_slab, plane, 2 - b, 2 - c, masks) for c in range(3)], axis=1
            )
            weights = kernel[a, b]
            forward_weights = weights.transpose(1, 0, 2).reshape(filt_local, 3 * chan_local)
            backward_weights = weights.reshape(3 * filt_local, chan_local)
            forward = forward + jnp.einsum(
                "fk,zkp->zfp", forward_weights, window, preferred_element_type=jnp.float32
            )
            backward = backward + jnp.einsum(
                "fk,zfp->zkp", backward_weights, grad_window, preferred_element_type=jnp.float32
            )
            joined = jnp.einsum(
                "zfp,zkp->fk", grad_full, window, preferred_element_type=jnp.float32
            )
            taps.append(joined.reshape(filt_local, 3, chan_local).transpose(1, 0, 2))
    output = lax.psum_scatter(forward, "chan", scatter_dimension=2, tiled=True).astype(jnp.bfloat16)
    input_grad = lax.psum_scatter(backward, "filt", scatter_dimension=1, tiled=True).astype(
        jnp.bfloat16
    )
    local_grad = jnp.stack(taps).reshape(3, 3, 3, filt_local, chan_local)
    total = lax.psum(local_grad, "space")
    cells = depth * lax.axis_size("space") * plane
    kernel_grad = total / jnp.sqrt(jnp.float32(cells))
    return (output, input_grad, kernel_grad)


def solution(mesh):
    placed = (
        P("space", ("chan", "filt"), None),
        P(None, None, None, "filt", "chan"),
        P("space", "filt", "chan"),
    )
    return jax.shard_map(
        body,
        mesh=mesh,
        in_specs=placed,
        out_specs=(
            P("space", "filt", "chan"),
            P("space", ("chan", "filt"), None),
            P(None, None, None, "filt", "chan"),
        ),
        check_vma=False,
    )
```

profile of v0, /device:TPU:12, one launch (start us, length us, event | category | flops | bytes accessed | tf_op | source)
XLA Modules:
  0.0 346.8 jit_solution(17022431209506651574)
XLA Ops:
  8.0 6.1 %all_gather.6 = bf16[1,256,512]{2,1,0:T(8,128)(2,1)S(1)} all-gather(bf16[1,128,512]{2,1,0:T(8,128)(2,1)} %param.3), channel_id=1, replica_groups=mesh['space'=8,'chan'=2,'filt'=2] {'filt'}, dimensions={1}, use_global_device_ids=true | all-gather | bytes 393216 | tf_op jit(solution)/shard_map/all_gather | solution.py:30
  14.2 2.4 collective-permute-start.1
  16.6 4.3 %collective-permute-start = (bf16[1,256,512]{2,1,0:T(8,128)(2,1)S(1)}, bf16[1,256,512]{2,1,0:T(8,128)(2,1)}, u32[]{:S(2)}, u32[]{:S(2)}) collective-permute-start(bf16[1,256,512]{2,1,0:T(8,128)(2,1)S(1)} %all_gather.6), channel_id=1, source_target_pairs={{0,4},{4,8},{8,12},{12,16},{16,20},{20,24},{24,28},{1,5},{5,9},{9,... | collective-permute-start | bytes 786440 | tf_op jit(solution)/shard_map/ppermute | solution.py:16
  20.9 2.3 all_gather.7
  23.2 2.5 collective-permute-start.2
  25.7 3.3 collective-permute-start.3
  29.1 3.2 fusion.87
  32.3 2.3 copy.42
  34.6 1.9 copy.43
  43.1 1.5 select_maximum_fusion.2
  45.3 1.6 select_maximum_fusion
  47.0 1.9 slice_multiply_fusion
  48.8 2.8 slice_multiply_fusion.26
  52.0 4.0 %slice_multiply_fusion.2 = (bf16[1,256,512]{2,1,0:T(8,128)(2,1)}, bf16[1,256,512]{2,1,0:T(8,128)(2,1)}, bf16[1,256,512]{2,1,0:T(8,128)(2,1)}, bf16[1,256,512]{2,...) fusion(bf16[3,256,546]{2,1,0:T(8,128)(2,1)S(1)} %select_maximum, ...), kind=kLoop, calls=%fused_computation.112 | loop fusion | flops 2228224 | bytes 8914944 | tf_op jit(solution)/shard_map/mul | solution.py:24
  63.6 1.8 broadcast_multiply_fusion.3
  65.4 1.3 pad_maximum_fusion.6
  69.1 1.6 fusion.13
  83.1 1.3 fusion.8
  88.3 1.3 fusion.4
  89.5 1.3 fusion.3
  92.1 1.3 fusion.1
  93.4 8.1 %copy.39 = f32[3,3,3,256,256]{4,3,2,1,0:T(8,128)} copy(f32[3,3,3,256,256]{3,4,2,1,0:T(8,128)} %bitcast.227) | data formatting | bytes 14155776 | tf_op jit(solution)/shard_map/reshape | solution.py:73
  105.0 227.7 %all-reduce.4.cloned.1.call-done = f32[3,3,3,256,256]{4,3,2,1,0:T(8,128)} async-done(((f32[3,3,3,256,256]{4,3,2,1,0:T(8,128)}), f32[3,3,3,256,256]{4,3,2,1,0:T(8,128)}) %all-reduce.4.cloned.1.call-update) | async-done | bytes 7077904 | tf_op jit(solution)/shard_map/psum | solution.py:74
  332.7 6.7 %broadcast_multiply_fusion = f32[3,3,3,256,256]{4,3,2,1,0:T(8,128)} fusion(f32[3,3,3,256,256]{4,3,2,1,0:T(8,128)} %all-reduce.4.cloned.1.call-done), kind=kLoop, calls=%fused_computation | loop fusion | flops 1769472 | bytes 14155776 | tf_op jit(solution)/shard_map/div | solution.py:76
  (173 shorter events, 38.4 us)
Async XLA Ops:
  8.0 93.5 %reduce-scatter.3.cloned.1.call-start = ((), (), s32[]{:S(2)}) async-start(), calls=%async_computation.2 | async-start | bytes 786432 | tf_op jit(solution)/shard_map/reduce_scatter | solution.py:69
  14.2 28.9 %collective-permute-start.1 = (bf16[1,256,512]{2,1,0:T(8,128)(2,1)S(1)}, bf16[1,256,512]{2,1,0:T(8,128)(2,1)}, u32[]{:S(2)}, u32[]{:S(2)}) collective-permute-start(bf16[1,256,512]{2,1,0:T(8,128)(2,1)S(1)} %all_gather.6), channel_id=1, source_target_pairs={{4,0},{8,4},{12,8},{16,12},{20,16},{24,20},{28,24},{5,1},{9,5},{13... | collective-permute-start | bytes 786440 | tf_op jit(solution)/shard_map/ppermute | solution.py:17
  16.6 26.5 %collective-permute-start = (bf16[1,256,512]{2,1,0:T(8,128)(2,1)S(1)}, bf16[1,256,512]{2,1,0:T(8,128)(2,1)}, u32[]{:S(2)}, u32[]{:S(2)}) collective-permute-start(bf16[1,256,512]{2,1,0:T(8,128)(2,1)S(1)} %all_gather.6), channel_id=1, source_target_pairs={{0,4},{4,8},{8,12},{12,16},{16,20},{20,24},{24,28},{1,5},{5,9},{9,... | collective-permute-start | bytes 786440 | tf_op jit(solution)/shard_map/ppermute | solution.py:16
  23.2 22.1 %collective-permute-start.2 = (bf16[1,256,512]{2,1,0:T(8,128)(2,1)S(1)}, bf16[1,256,512]{2,1,0:T(8,128)(2,1)}, u32[]{:S(2)}, u32[]{:S(2)}) collective-permute-start(bf16[1,256,512]{2,1,0:T(8,128)(2,1)S(1)} %all_gather.7), channel_id=1, source_target_pairs={{0,4},{4,8},{8,12},{12,16},{16,20},{20,24},{24,28},{1,5},{5,9},{9,... | collective-permute-start | bytes 786440 | tf_op jit(solution)/shard_map/ppermute | solution.py:16
  25.7 19.6 %collective-permute-start.3 = (bf16[1,256,512]{2,1,0:T(8,128)(2,1)S(1)}, bf16[1,256,512]{2,1,0:T(8,128)(2,1)}, u32[]{:S(2)}, u32[]{:S(2)}) collective-permute-start(bf16[1,256,512]{2,1,0:T(8,128)(2,1)S(1)} %all_gather.7), channel_id=1, source_target_pairs={{4,0},{8,4},{12,8},{16,12},{20,16},{24,20},{28,24},{5,1},{9,5},{13... | collective-permute-start | bytes 786440 | tf_op jit(solution)/shard_map/ppermute | solution.py:17
  32.3 6.1 %copy-start.15 = (bf16[1,1,3,256,256]{4,3,2,1,0:T(8,128)(2,1)}, bf16[1,1,3,256,256]{4,3,2,1,0:T(8,128)(2,1)S(1)}, u32[]{:S(2)}) copy-start(bf16[1,1,3,256,256]{4,3,2,1,0:T(8,128)(2,1)S(1)} %get-tuple-element.17) | copy-start | bytes 1179652
  32.3 6.1 %copy-start.17 = (bf16[1,1,3,256,256]{4,3,2,1,0:T(8,128)(2,1)}, bf16[1,1,3,256,256]{4,3,2,1,0:T(8,128)(2,1)S(1)}, u32[]{:S(2)}) copy-start(bf16[1,1,3,256,256]{4,3,2,1,0:T(8,128)(2,1)S(1)} %get-tuple-element.18) | copy-start | bytes 1179652
  32.3 6.1 %copy-start.13 = (bf16[1,1,3,256,256]{4,3,2,1,0:T(8,128)(2,1)}, bf16[1,1,3,256,256]{4,3,2,1,0:T(8,128)(2,1)S(1)}, u32[]{:S(2)}) copy-start(bf16[1,1,3,256,256]{4,3,2,1,0:T(8,128)(2,1)S(1)} %get-tuple-element.16) | copy-start | bytes 1179652
  32.3 7.0 %copy-start.11 = (bf16[1,1,3,256,256]{4,3,2,1,0:T(8,128)(2,1)}, bf16[1,1,3,256,256]{4,3,2,1,0:T(8,128)(2,1)S(1)}, u32[]{:S(2)}) copy-start(bf16[1,1,3,256,256]{4,3,2,1,0:T(8,128)(2,1)S(1)} %get-tuple-element.15) | copy-start | bytes 1179652
  32.3 7.9 %copy-start.9 = (bf16[1,1,3,256,256]{4,3,2,1,0:T(8,128)(2,1)}, bf16[1,1,3,256,256]{4,3,2,1,0:T(8,128)(2,1)S(1)}, u32[]{:S(2)}) copy-start(bf16[1,1,3,256,256]{4,3,2,1,0:T(8,128)(2,1)S(1)} %get-tuple-element.14) | copy-start | bytes 1179652
  32.3 8.8 %copy-start.7 = (bf16[1,1,3,256,256]{4,3,2,1,0:T(8,128)(2,1)}, bf16[1,1,3,256,256]{4,3,2,1,0:T(8,128)(2,1)S(1)}, u32[]{:S(2)}) copy-start(bf16[1,1,3,256,256]{4,3,2,1,0:T(8,128)(2,1)S(1)} %get-tuple-element.13) | copy-start | bytes 1179652
  32.3 9.8 %copy-start.5 = (bf16[1,1,3,256,256]{4,3,2,1,0:T(8,128)(2,1)}, bf16[1,1,3,256,256]{4,3,2,1,0:T(8,128)(2,1)S(1)}, u32[]{:S(2)}) copy-start(bf16[1,1,3,256,256]{4,3,2,1,0:T(8,128)(2,1)S(1)} %get-tuple-element.12) | copy-start | bytes 1179652
  45.3 21.8 %copy-start.21 = (bf16[1,256,512]{2,1,0:T(8,128)(2,1)}, bf16[1,256,512]{2,1,0:T(8,128)(2,1)S(1)}, u32[]{:S(2)}) copy-start(bf16[1,256,512]{2,1,0:T(8,128)(2,1)S(1)} %get-tuple-element.60) | copy-start | bytes 786436
  48.8 2.8 copy-start.35
  51.6 15.5 %copy-start.23 = (bf16[1,256,512]{2,1,0:T(8,128)(2,1)}, bf16[1,256,512]{2,1,0:T(8,128)(2,1)S(1)}, u32[]{:S(2)}) copy-start(bf16[1,256,512]{2,1,0:T(8,128)(2,1)S(1)} %get-tuple-element.45) | copy-start | bytes 786436
  51.6 15.5 %copy-start.25 = (bf16[1,256,512]{2,1,0:T(8,128)(2,1)}, bf16[1,256,512]{2,1,0:T(8,128)(2,1)S(1)}, u32[]{:S(2)}) copy-start(bf16[1,256,512]{2,1,0:T(8,128)(2,1)S(1)} %get-tuple-element.80) | copy-start | bytes 786436
  68.9 34.4 %reduce-scatter.5.cloned.1.call-start = ((), (), s32[]{:S(2)}) async-start(), calls=%async_computation.3 | async-start | bytes 786432 | tf_op jit(solution)/shard_map/reduce_scatter | solution.py:70
  69.1 1.7 copy-start.19
  69.1 1.7 copy-start.46
  83.1 249.6 %all-reduce.4.cloned.1.call-start = ((), (), s32[]{:S(2)}) async-start(), calls=%async_computation.4 | async-start | bytes 14155776 | tf_op jit(solution)/shard_map/psum | solution.py:74
  84.4 2.6 copy-start.2
  85.7 2.6 copy-start.1
  87.0 2.6 copy-start.4
  88.3 2.6 copy-start.3
  (43 other events, 48.9 us)
Sparse Core Ops, SparseCore 0:
  69.0 9.0 reduce-scatter.2
  83.2 15.4 reduce-scatter.4
Sparse Core Ops, SparseCore 1:
  101.6 231.0 all-reduce.3
where the time goes:
time: 351 us; the launch traced here: 347 us
  waiting for transfers between devices  228 us (65%)
  local copies, waits for them, and re-layouts  33.5 us (10%)
  other arithmetic  26.6 us (8%)
  matrix products  21.7 us (6%)
  between operations  16 us (5%)
  starting transfers between devices  12.9 us (4%)
  blocking collectives  8.42 us (2%)
    psum x1, waiting for transfers between devices, body(): total = lax.psum(local_grad, 'space')  228 us
    unnamed x131, local copies, waits for them, and re-layouts  22.2 us
    dot_general x9, matrix products, body(): jnp.einsum('zfp,zkp->fk', grad_full, window, preferred_element_type=jnp.f...  11.5 us
    mul x5, other arithmetic, plane_window(): return widened[:, :, begin:begin + plane] * masks[col_step]  11.1 us
    reshape x1, local copies, waits for them, and re-layouts, body(): local_grad = jnp.stack(taps).reshape(3, 3, 3, filt_local, chan_local)  8.07 us
  transfers between devices with their start and end apart: 7, of which 1 were waited for; matrix products, arithmetic and copies ran while one was open for 13% of the time, Pallas kernels for 0%

commit v1 on v0

v1 whole, which is shorter than its diff:
```python
import functools
import math

import jax
import jax.numpy as jnp
from jax import lax
from jax.experimental import pallas as pl
from jax.experimental.pallas import tpu as pltpu
from jax.sharding import PartitionSpec as P

W = 16
MESH = pl.DeviceIdType.MESH


def shifted_copies(t, store):
    cells = t.shape[0]
    column = lax.broadcasted_iota(jnp.int32, t.shape, 0) % W
    store(0, jnp.where(column >= 1, pltpu.roll(t, 1, 0), 0.0).astype(jnp.bfloat16))
    store(1, t.astype(jnp.bfloat16))
    store(2, jnp.where(column <= W - 2, pltpu.roll(t, cells - 1, 0), 0.0).astype(jnp.bfloat16))


def kernel(
    sizes, act_ref, w_hbm, grad_ref, out_ref, ig_ref, kg_hbm,
    actg, gradg, wide, gwide, w, facc, bacc, fpart, bpart, frecv, brecv, stage,
    w_sem, kg_sem, az_send, ay_send, ax_send, gz_send, gy_send, gc_send,
    a_recv, g_recv, f_send, f_recv, b_send, b_recv,
):
    S, NX, NZ, NY = sizes
    cb, cells = act_ref.shape[1:]
    filters, half = grad_ref.shape[1:]
    chans = NX * cb
    s = lax.axis_index("space")
    c = lax.axis_index("chan")
    x = lax.axis_index("filt")
    z, y = s // NY, s % NY
    oy = (y + 1) % NY
    f32 = jnp.float32

    def remote(src, dst, send, recv, device):
        return pltpu.make_async_remote_copy(
            src_ref=src, dst_ref=dst, send_sem=send, recv_sem=recv,
            device_id=device, device_id_type=MESH,
        )

    zpeers = [{"space": ((z + d) % NZ) * NY + y} for d in range(1, NZ)]
    ypeer = {"space": z * NY + oy}
    xpeers = [{"filt": (x + d) % NX} for d in range(1, NX)]
    cpeer = {"chan": 1 - c}
    barrier = pltpu.get_barrier_semaphore()
    for peer in zpeers + xpeers + [ypeer, cpeer]:
        pl.semaphore_signal(barrier, inc=1, device_id=peer, device_id_type=MESH)
    pl.semaphore_wait(barrier, len(zpeers) + len(xpeers) + 2)

    def a_slot(plane, part):
        return actg.at[plane, pl.ds(pl.multiple_of(part * cb, cb), cb), :]

    def g_slot(plane, part):
        return gradg.at[plane + 1, :, pl.ds(pl.multiple_of(part * half, half), half)]

    def a_z(d):
        return remote(act_ref.at[0], a_slot(s, x), az_send.at[d - 1], a_recv.at[s * NX + x], zpeers[d - 1])

    def g_z(d):
        return remote(grad_ref.at[0], g_slot(s, c), gz_send.at[d - 1], g_recv.at[s * 2 + c], zpeers[d - 1])

    def a_y(k, plane, src):
        return remote(src, a_slot(plane, x), ay_send.at[k], a_recv.at[plane * NX + x], ypeer)

    def g_y(k, plane, src):
        return remote(src, g_slot(plane, c), gy_send.at[k], g_recv.at[plane * 2 + c], ypeer)

    def a_x(k, e, plane, src):
        return remote(
            src, a_slot(plane, x), ax_send.at[k * (NX - 1) + e - 1], a_recv.at[plane * NX + x], xpeers[e - 1]
        )

    def g_c(k, plane, src):
        return remote(src, g_slot(plane, c), gc_send.at[k], g_recv.at[plane * 2 + c], cpeer)

    def a_wait(plane, part):
        a_z_like = remote(
            act_ref.at[0], a_slot(plane, part), az_send.at[0], a_recv.at[plane * NX + part], ypeer
        )
        a_z_like.wait_recv()

    def g_wait(plane, part):
        remote(
            grad_ref.at[0], g_slot(plane, part), gz_send.at[0], g_recv.at[plane * 2 + part], ypeer
        ).wait_recv()

    def mine(d):
        return ((z + d) % NZ) * NY + y

    def other(d):
        return ((z + d) % NZ) * NY + oy

    for d in range(1, NZ):
        g_z(d).start()
        a_z(d).start()
    g_y(0, s, grad_ref.at[0]).start()
    a_y(0, s, act_ref.at[0]).start()
    for e in range(1, NX):
        a_x(0, e, s, act_ref.at[0]).start()
    g_c(0, s, grad_ref.at[0]).start()
    w_copy = pltpu.make_async_copy(w_hbm, w, w_sem)
    w_copy.start()
    actg[s, pl.ds(pl.multiple_of(x * cb, cb), cb), :] = act_ref[0]
    gradg[s + 1, :, pl.ds(pl.multiple_of(c * half, half), half)] = grad_ref[0]
    for end in (0, S + 1):
        gradg[end] = jnp.zeros((filters, cells), jnp.bfloat16)
        wide[end] = jnp.zeros(wide.shape[1:], jnp.bfloat16)

    @pl.loop(1, S + 1)
    def _(j):
        for k in range(3):
            wide[j, k, 0:W, :] = jnp.zeros((W, chans), jnp.bfloat16)
            wide[j, k, W + cells : 2 * W + cells, :] = jnp.zeros((W, chans), jnp.bfloat16)

    for j in range(3):
        for k in range(3):
            gwide[j, k, 0:W, :] = jnp.zeros((W, filters), jnp.bfloat16)
            gwide[j, k, W + cells : 2 * W + cells, :] = jnp.zeros((W, filters), jnp.bfloat16)

    @pl.loop(1, NZ)
    def _(d):
        plane = mine(d)
        g_wait(plane, c)
        g_y(d, plane, g_slot(plane, c)).start()
        g_c(d, plane, g_slot(plane, c)).start()
        a_wait(plane, x)
        a_y(d, plane, a_slot(plane, x)).start()
        for e in range(1, NX):
            a_x(d, e, plane, a_slot(plane, x)).start()

    @pl.loop(0, NZ)
    def _(d):
        plane = other(d)
        a_wait(plane, x)
        for e in range(1, NX):
            a_x(NZ + d, e, plane, a_slot(plane, x)).start()
        g_wait(plane, c)
        g_c(NZ + d, plane, g_slot(plane, c)).start()

    @pl.loop(0, S)
    def _(i):
        plane = (s + i) % S
        g_wait(plane, 1 - c)
        for e in range(1, NX):
            a_wait(plane, (x + e) % NX)

    @pl.loop(0, S)
    def _(i):
        def store(k, value):
            wide[i + 1, k, W : W + cells, :] = value

        shifted_copies(actg[i].astype(f32).T, store)

    @pl.loop(0, 3)
    def _(j):
        def store(k, value):
            gwide[j, k, W : W + cells, :] = value

        shifted_copies(gradg[s + j].astype(f32).T, store)

    w_copy.wait()
    facc[...] = jnp.zeros_like(facc)
    bacc[...] = jnp.zeros_like(bacc)

    @pl.loop(0, 9)
    def _(i):
        a, b = i // 3, i % 3
        total = None
        for k in range(3):
            rows = wide[s + a, k, pl.ds(pl.multiple_of(b * W, W), cells), :]
            term = lax.dot_general(rows, w[a, b, k], (((1,), (1,)), ((), ())), preferred_element_type=f32)
            total = term if total is None else total + term
        facc[...] += total

    fpart[...] = facc[...].T
    f_copy = remote(
        fpart.at[:, pl.ds(pl.multiple_of((1 - c) * half, half), half)], frecv, f_send, f_recv, cpeer
    )
    f_copy.start()

    @pl.loop(0, 9)
    def _(i):
        a, b = i // 3, i % 3
        total = None
        for k in range(3):
            rows = gwide[2 - a, 2 - k, pl.ds(pl.multiple_of((2 - b) * W, W), cells), :]
            term = jnp.dot(rows, w[a, b, k], preferred_element_type=f32)
            total = term if total is None else total + term
        bacc[...] += total

    bpart[...] = bacc[...].T

    def b_copy(e):
        to = (x + e) % NX
        return remote(
            bpart.at[pl.ds(pl.multiple_of(to * cb, cb), cb), :],
            brecv.at[e - 1], b_send.at[e - 1], b_recv.at[e - 1], xpeers[e - 1],
        )

    for e in range(1, NX):
        b_copy(e).start()

    scale = 1.0 / math.sqrt(S * cells)
    group = 4

    def kg_copy(i, j):
        return pltpu.make_async_copy(stage.at[i, j], kg_hbm.at[2 - j, i // 3, i % 3], kg_sem.at[i * 3 + j])

    @pl.loop(0, 9)
    def _(i):
        b, k = i // 3, i % 3

        @pl.loop(0, S // group)
        def _(q):
            total = None
            for n in range(group):
                j = q * group + n
                rows = wide[j + 1, k, pl.ds(pl.multiple_of(b * W, W), cells), :]
                grads = gradg[pl.ds(j, 3)].reshape(3 * filters, cells)
                term = jnp.dot(grads, rows, preferred_element_type=f32)
                total = term if total is None else total + term
            total = (total * scale).reshape(3, filters, chans)

            @pl.when(q == 0)
            def _():
                stage[i] = total

            @pl.when(q > 0)
            def _():
                stage[i] += total

        for j in range(3):
            kg_copy(i, j).start()

    f_copy.wait()
    out_ref[0] = (fpart[:, pl.ds(pl.multiple_of(c * half, half), half)] + frecv[...]).astype(jnp.bfloat16)
    own = bpart[pl.ds(pl.multiple_of(x * cb, cb), cb), :]
    for e in range(1, NX):
        b_copy(e).wait()
        own = own + brecv[e - 1]
    ig_ref[0] = own.astype(jnp.bfloat16)

    for d in range(1, NZ):
        a_z(d).wait_send()
        g_z(d).wait_send()

    @pl.loop(0, NZ)
    def _(d):
        a_y(d, mine(d), a_slot(mine(d), x)).wait_send()
        g_y(d, mine(d), g_slot(mine(d), c)).wait_send()

    @pl.loop(0, S)
    def _(k):
        for e in range(1, NX):
            a_x(k, e, s, a_slot(s, x)).wait_send()
        g_c(k, s, g_slot(s, c)).wait_send()

    @pl.loop(0, 9)
    def _(i):
        for j in range(3):
            kg_copy(i, j).wait()


def body(activation, weights, out_grad):
    S = lax.axis_size("space")
    NX = lax.axis_size("filt")
    NY = 2
    NZ = S // NY
    cb, cells = activation.shape[1:]
    filters, half = out_grad.shape[1:]
    chans = NX * cb
    bf16, f32 = jnp.bfloat16, jnp.float32
    dma = pltpu.SemaphoreType.DMA
    vmem = pl.BlockSpec(memory_space=pltpu.VMEM)
    hbm = pl.BlockSpec(memory_space=pl.ANY)
    return pl.pallas_call(
        functools.partial(kernel, (S, NX, NZ, NY)),
        out_shape=(
            jax.ShapeDtypeStruct(out_grad.shape, bf16),
            jax.ShapeDtypeStruct(activation.shape, bf16),
            jax.ShapeDtypeStruct(weights.shape, f32),
        ),
        in_specs=[vmem, hbm, vmem],
        out_specs=(vmem, vmem, hbm),
        scratch_shapes=[
            pltpu.VMEM((S, chans, cells), bf16),
            pltpu.VMEM((S + 2, filters, cells), bf16),
            pltpu.VMEM((S + 2, 3, cells + 2 * W, chans), bf16),
            pltpu.VMEM((3, 3, cells + 2 * W, filters), bf16),
            pltpu.VMEM(weights.shape, bf16),
            pltpu.VMEM((cells, filters), f32),
            pltpu.VMEM((cells, chans), f32),
            pltpu.VMEM((filters, cells), f32),
            pltpu.VMEM((chans, cells), f32),
            pltpu.VMEM((filters, half), f32),
            pltpu.VMEM((NX - 1, cb, cells), f32),
            pltpu.VMEM((9, 3, filters, chans), f32),
            dma, dma((27,)),
            dma((NZ - 1,)), dma((NZ,)), dma((S * (NX - 1),)),
            dma((NZ - 1,)), dma((NZ,)), dma((S,)),
            dma((S * NX,)), dma((S * 2,)),
            dma, dma, dma((NX - 1,)), dma((NX - 1,)),
        ],
        compiler_params=pltpu.CompilerParams(
            collective_id=0, has_side_effects=True, vmem_limit_bytes=56 * 1024 * 1024
        ),
    )(activation, weights, out_grad)


def solution(mesh):
    placed = (
        P("space", ("chan", "filt"), None),
        P(None, None, None, "filt", "chan"),
        P("space", "filt", "chan"),
    )
    return jax.shard_map(
        body,
        mesh=mesh,
        in_specs=placed,
        out_specs=(
            P("space", "filt", "chan"),
            P("space", ("chan", "filt"), None),
            P(None, None, None, "filt", "chan"),
        ),
        check_vma=False,
    )
```

time: 351 us -> 90.9 us (0.26); the launches traced: 347 us -> 90.7 us
  waiting for transfers between devices: 228 us -> 0 us
  Pallas kernels: 0 us -> 80.2 us
  other arithmetic: 26.6 us -> 0 us
  local copies, waits for them, and re-layouts: 33.5 us -> 9.86 us
  matrix products: 21.7 us -> 0 us
  between operations: 16 us -> 0.64 us
  starting transfers between devices: 12.9 us -> 0 us
  blocking collectives: 8.42 us -> 0 us
    psum x1 -> x0, waiting for transfers between devices: 228 us -> none  [body(): total = lax.psum(local_grad, 'space')]
    pallas_call x0 -> x1, Pallas kernels: none -> 80.2 us  [body(): pl.pallas_call(functools.partial(kernel, (S, NX, NZ, NY)), out_shape=(jax...]
    dot_general x27 -> x0, matrix products: 21.7 us -> none  [the longest x9 11.5 us: body(): jnp.einsum('zfp,zkp->fk', grad_full, window, preferred_element_type=jnp.f...]
    ppermute x4 -> x0, starting transfers between devices: 12.6 us -> none  [the longest x2 6.85 us: padded(): before = lax.ppermute(last, axis, up)]
    unnamed x131 -> x3, local copies, waits for them, and re-layouts: 22.2 us -> 9.86 us
    mul x5 -> x0, other arithmetic: 11.1 us -> none  [plane_window(): return widened[:, :, begin:begin + plane] * masks[col_step]]
    all_gather x2 -> x0, blocking collectives: 8.42 us -> none  [the longest x1 6.13 us: body(): panels = lax.all_gather(activation, 'filt', axis=1, tiled=True)]
    reshape x1 -> x0, local copies, waits for them, and re-layouts: 8.07 us -> none  [body(): local_grad = jnp.stack(taps).reshape(3, 3, 3, filt_local, chan_local)]
  transfers between devices with their start and end apart: 7 -> 0, of which waited for: 1 -> 0; matrix products, arithmetic and copies ran while one was open for 13% -> 0% of each run, Pallas kernels for 0% -> 0%
where the time goes in v1:
time: 90.9 us; the launch traced here: 90.7 us
  Pallas kernels  80.2 us (88%)
  local copies, waits for them, and re-layouts  9.86 us (11%)
    pallas_call x1, Pallas kernels, body(): pl.pallas_call(functools.partial(kernel, (S, NX, NZ, NY)), out_shape=(jax...  80.2 us
    unnamed x3, local copies, waits for them, and re-layouts  9.86 us

profile of v1, /device:TPU:12, one launch (start us, length us, event | category | flops | bytes accessed | tf_op | source)
XLA Modules:
  0.0 90.7 jit_solution(8187080900235985519)
XLA Ops:
  0.6 80.2 %shard_map.58 = (bf16[1,256,256]{2,1,0:T(8,128)(2,1)}, bf16[1,128,512]{2,1,0:T(8,128)(2,1)}, f32[3,3,3,256,256]{4,3,2,1,0:T(8,128)}) custom-call(bf16[1,128,512]{2,1,0:T(8,128)(2,1)} %act_ref.1, bf16[3,3,3,256,256]{4,3,2,1,0:T(8,128)(2,1)} %w_hbm.1, bf16[1,256,256]{2,1,0:T(8,128)(2,1)} %grad_ref.1), custom_call_target="tpu_custom_call" | custom-call | tf_op jit(solution)/shard_map/pallas_call | solution.py:281
  80.9 1.6 %copy.9 = bf16[1,256,256]{2,1,0:T(8,128)(2,1)} copy(bf16[1,256,256]{2,1,0:T(8,128)(2,1)} %get-tuple-element.6) | data formatting | bytes 262144
  82.4 1.6 %copy.10 = bf16[1,128,512]{2,1,0:T(8,128)(2,1)} copy(bf16[1,128,512]{2,1,0:T(8,128)(2,1)} %get-tuple-element.7) | data formatting | bytes 262144
  84.0 6.7 %copy.11 = f32[3,3,3,256,256]{4,3,2,1,0:T(8,128)} copy(f32[3,3,3,256,256]{4,3,2,1,0:T(8,128)} %get-tuple-element.8) | data formatting | bytes 14155776

commit v2 on v0

v2 whole, which is shorter than its diff:
```python
import functools
import math

import jax
import jax.numpy as jnp
from jax import lax
from jax.experimental import pallas as pl
from jax.experimental.pallas import tpu as pltpu
from jax.sharding import PartitionSpec as P

W = 16
MESH = pl.DeviceIdType.MESH


def shifted_copies(t, store):
    cells = t.shape[0]
    column = lax.broadcasted_iota(jnp.int32, t.shape, 0) % W
    store(0, jnp.where(column >= 1, pltpu.roll(t, 1, 0), 0.0).astype(jnp.bfloat16))
    store(1, t.astype(jnp.bfloat16))
    store(2, jnp.where(column <= W - 2, pltpu.roll(t, cells - 1, 0), 0.0).astype(jnp.bfloat16))


def kernel(
    sizes, act_ref, w_hbm, grad_ref, out_ref, ig_ref, acc,
    actg, gradg, wide, gwide, w, facc, bacc, fpart, bpart, frecv, brecv,
    w_sem, az_send, ay_send, ax_send, gz_send, gy_send, gc_send,
    a_recv, g_recv, f_send, f_recv, b_send, b_recv,
):
    S, NX, NZ, NY = sizes
    cb, cells = act_ref.shape[1:]
    filters, half = grad_ref.shape[1:]
    chans = NX * cb
    s = lax.axis_index("space")
    c = lax.axis_index("chan")
    x = lax.axis_index("filt")
    z, y = s // NY, s % NY
    oy = 1 - y
    f32, bf16 = jnp.float32, jnp.bfloat16

    def remote(src, dst, send, recv, device):
        return pltpu.make_async_remote_copy(
            src_ref=src, dst_ref=dst, send_sem=send, recv_sem=recv,
            device_id=device, device_id_type=MESH,
        )

    def signal(device):
        pl.semaphore_signal(barrier, inc=1, device_id=device, device_id_type=MESH)

    def a_slot(plane, part):
        return actg.at[plane, pl.ds(pl.multiple_of(part * cb, cb), cb), :]

    def g_slot(plane, part):
        return gradg.at[plane + 1, :, pl.ds(pl.multiple_of(part * half, half), half)]

    ypeer = {"space": z * NY + oy}
    xpeers = [{"filt": (x + e) % NX} for e in range(1, NX)]
    cpeer = {"chan": 1 - c}

    def a_copy(plane, send, device):
        slot = a_slot(plane, x)
        return remote(slot, slot, send, a_recv.at[plane * NX + x], device)

    def g_copy(plane, send, device):
        slot = g_slot(plane, c)
        return remote(slot, slot, send, g_recv.at[plane * 2 + c], device)

    def a_wait(plane, part):
        slot = a_slot(plane, part)
        remote(slot, slot, ay_send.at[0], a_recv.at[plane * NX + part], ypeer).wait_recv()

    def g_wait(plane, part):
        slot = g_slot(plane, part)
        remote(slot, slot, gy_send.at[0], g_recv.at[plane * 2 + part], ypeer).wait_recv()

    def a_z(zz, way):
        to = {"space": (z + way) * NY + y}
        return a_copy(zz * NY + y, az_send.at[(way + 1) // 2 * NZ + zz], to)

    def g_z(zz, way):
        to = {"space": (z + way) * NY + y}
        return g_copy(zz * NY + y, gz_send.at[(way + 1) // 2 * NZ + zz], to)

    def a_y(zz):
        return a_copy(zz * NY + y, ay_send.at[zz], ypeer)

    def g_y(zz):
        return g_copy(zz * NY + y, gy_send.at[zz], ypeer)

    def a_x(plane, e):
        return a_copy(plane, ax_send.at[plane * (NX - 1) + e - 1], xpeers[e - 1])

    def g_c(plane):
        return g_copy(plane, gc_send.at[plane], cpeer)

    def start_x(plane):
        for e in range(1, NX):
            a_x(plane, e).start()

    def inside(zz):
        return (zz >= 0) & (zz < NZ)

    def at_distance(d, run):
        @pl.when(inside(z - d))
        def _():
            run(z - d, -1)

        @pl.when((d > 0) & inside(z + d))
        def _():
            run(z + d, 1)

    actg[s, pl.ds(pl.multiple_of(x * cb, cb), cb), :] = act_ref[0]
    gradg[s + 1, :, pl.ds(pl.multiple_of(c * half, half), half)] = grad_ref[0]
    barrier = pltpu.get_barrier_semaphore()
    for way in (-1, 1):
        @pl.when(inside(z + way))
        def _():
            signal({"space": (z + way) * NY + y})
    for peer in [ypeer, cpeer] + xpeers:
        signal(peer)
    beside = (z + NZ - 1) // NZ + (2 * NZ - 2 - z) // NZ
    pl.semaphore_wait(barrier, NX + 1 + beside)

    for way in (-1, 1):
        @pl.when(inside(z + way))
        def _():
            a_z(z, way).start()
    a_y(z).start()
    start_x(s)
    for way in (-1, 1):
        @pl.when(inside(z + way))
        def _():
            g_z(z, way).start()
    g_y(z).start()
    g_c(s).start()
    w_copy = pltpu.make_async_copy(w_hbm, w, w_sem)
    w_copy.start()

    for end in (0, S + 1):
        gradg[end] = jnp.zeros((filters, cells), bf16)
        wide[end] = jnp.zeros(wide.shape[1:], bf16)

    @pl.loop(1, S + 1)
    def _(j):
        for k in range(3):
            wide[j, k, 0:W, :] = jnp.zeros((W, chans), bf16)
            wide[j, k, W + cells : 2 * W + cells, :] = jnp.zeros((W, chans), bf16)

    for j in range(3):
        for k in range(3):
            gwide[j, k, 0:W, :] = jnp.zeros((W, filters), bf16)
            gwide[j, k, W + cells : 2 * W + cells, :] = jnp.zeros((W, filters), bf16)

    @pl.loop(0, 27)
    def _(i):
        acc[i // 9, i // 3 % 3, i % 3] = jnp.zeros((filters, chans), f32)

    facc[...] = jnp.zeros_like(facc)
    bacc[...] = jnp.zeros_like(bacc)
    w_copy.wait()

    def b_copy(e):
        to = (x + e) % NX
        return remote(
            bpart.at[pl.ds(pl.multiple_of(to * cb, cb), cb), :],
            brecv.at[e - 1], b_send.at[e - 1], b_recv.at[e - 1], xpeers[e - 1],
        )

    f_copy = remote(
        fpart.at[:, pl.ds(pl.multiple_of((1 - c) * half, half), half)], frecv, f_send, f_recv, cpeer
    )

    def backward():
        @pl.loop(0, 3)
        def _(j):
            def store(k, value):
                gwide[j, k, W : W + cells, :] = value

            shifted_copies(gradg[s + j].astype(f32).T, store)

        @pl.loop(0, 9)
        def _(i):
            a, b = i // 3, i % 3
            total = None
            for k in range(3):
                rows = gwide[2 - a, 2 - k, pl.ds(pl.multiple_of((2 - b) * W, W), cells), :]
                term = jnp.dot(rows, w[a, b, k], preferred_element_type=f32)
                total = term if total is None else total + term
            bacc[...] += total

        bpart[...] = bacc[...].T
        for e in range(1, NX):
            b_copy(e).start()

    def forward():
        @pl.loop(0, 9)
        def _(i):
            a, b = i // 3, i % 3
            total = None
            for k in range(3):
                rows = wide[s + a, k, pl.ds(pl.multiple_of(b * W, W), cells), :]
                term = lax.dot_general(rows, w[a, b, k], (((1,), (1,)), ((), ())), preferred_element_type=f32)
                total = term if total is None else total + term
            facc[...] += total

        fpart[...] = facc[...].T
        f_copy.start()

    def prepare(zz):
        @pl.loop(0, NY)
        def _(i):
            plane = zz * NY + i
            for e in range(1, NX):
                a_wait(plane, (x + e) % NX)

            def store(k, value):
                wide[plane + 1, k, W : W + cells, :] = value

            shifted_copies(actg[plane].astype(f32).T, store)

    scale = 1.0 / math.sqrt(S * cells)

    def filter_grad(zz):
        @pl.loop(0, 9)
        def _(i):
            b, k = i // 3, i % 3
            total = None
            for n in range(NY):
                j = zz * NY + n
                rows = wide[j + 1, k, pl.ds(pl.multiple_of(b * W, W), cells), :]
                grads = gradg[pl.ds(j, 3)].reshape(3 * filters, cells)
                term = jnp.dot(grads, rows, preferred_element_type=f32)
                total = term if total is None else total + term
            for j in range(3):
                acc[2 - j, b, k] += total[j * filters : (j + 1) * filters] * scale

    def relay(zz, way, wait, along, across, last):
        plane = zz * NY + y
        wait(plane)

        @pl.when(inside(z - way))
        def _():
            along(zz, -way).start()

        across(zz).start()
        last(plane)

    def pass_on(zz, wait, last):
        plane = zz * NY + oy
        wait(plane)
        last(plane)

    def a_own(plane):
        a_wait(plane, x)

    def g_own(plane):
        g_wait(plane, c)

    def start_c(plane):
        g_c(plane).start()

    def core_halves(zz, way):
        for n in range(NY):
            g_wait(zz * NY + n, 1 - c)

    @pl.loop(1, NZ + 2)
    def _(d):
        at_distance(d - 1, lambda zz, way: pass_on(zz, a_own, start_x))
        at_distance(d, lambda zz, way: relay(zz, way, a_own, a_z, a_y, start_x))
        at_distance(d - 1, lambda zz, way: pass_on(zz, g_own, start_c))
        at_distance(d, lambda zz, way: relay(zz, way, g_own, g_z, g_y, start_c))
        at_distance(d - 1, core_halves)

        @pl.when(d == 2)
        def _():
            backward()

        @pl.when(d >= 2)
        def _():
            at_distance(d - 2, lambda zz, way: prepare(zz))

        @pl.when(d == 3)
        def _():
            forward()

        @pl.when(d >= 2)
        def _():
            at_distance(d - 2, lambda zz, way: filter_grad(zz))

    f_copy.wait()
    out_ref[0] = (fpart[:, pl.ds(pl.multiple_of(c * half, half), half)] + frecv[...]).astype(bf16)
    own = bpart[pl.ds(pl.multiple_of(x * cb, cb), cb), :]
    for e in range(1, NX):
        b_copy(e).wait()
        own = own + brecv[e - 1]
    ig_ref[0] = own.astype(bf16)

    @pl.loop(0, NZ)
    def _(zz):
        for way in (-1, 1):
            @pl.when(inside(z + way) & ((z - zz) * way >= 0))
            def _():
                a_z(zz, way).wait_send()
                g_z(zz, way).wait_send()
        a_y(zz).wait_send()
        g_y(zz).wait_send()

    @pl.loop(0, S)
    def _(plane):
        for e in range(1, NX):
            a_x(plane, e).wait_send()
        g_c(plane).wait_send()


def body(activation, weights, out_grad):
    S = lax.axis_size("space")
    NX = lax.axis_size("filt")
    NY = 2
    NZ = S // NY
    cb, cells = activation.shape[1:]
    filters, half = out_grad.shape[1:]
    chans = NX * cb
    bf16, f32 = jnp.bfloat16, jnp.float32
    dma = pltpu.SemaphoreType.DMA
    vmem = pl.BlockSpec(memory_space=pltpu.VMEM)
    hbm = pl.BlockSpec(memory_space=pl.ANY)
    shapes = ((out_grad.shape, bf16), (activation.shape, bf16), (weights.shape, f32))
    results = pl.pallas_call(
        functools.partial(kernel, (S, NX, NZ, NY)),
        out_shape=tuple(pltpu.VMEM(*shape) for shape in shapes),
        in_specs=[vmem, hbm, vmem],
        out_specs=(vmem, vmem, vmem),
        scratch_shapes=[
            pltpu.VMEM((S, chans, cells), bf16),
            pltpu.VMEM((S + 2, filters, cells), bf16),
            pltpu.VMEM((S + 2, 3, cells + 2 * W, chans), bf16),
            pltpu.VMEM((3, 3, cells + 2 * W, filters), bf16),
            pltpu.VMEM(weights.shape, bf16),
            pltpu.VMEM((cells, filters), f32),
            pltpu.VMEM((cells, chans), f32),
            pltpu.VMEM((filters, cells), f32),
            pltpu.VMEM((chans, cells), f32),
            pltpu.VMEM((filters, half), f32),
            pltpu.VMEM((NX - 1, cb, cells), f32),
            dma,
            dma((2 * NZ,)), dma((NZ,)), dma((S * (NX - 1),)),
            dma((2 * NZ,)), dma((NZ,)), dma((S,)),
            dma((S * NX,)), dma((S * 2,)),
            dma, dma, dma((NX - 1,)), dma((NX - 1,)),
        ],
        compiler_params=pltpu.CompilerParams(
            collective_id=0, has_side_effects=True, vmem_limit_bytes=50 * 1024 * 1024
        ),
    )(activation, weights, out_grad)
    return results


def solution(mesh):
    placed = (
        P("space", ("chan", "filt"), None),
        P(None, None, None, "filt", "chan"),
        P("space", "filt", "chan"),
    )
    return jax.shard_map(
        body,
        mesh=mesh,
        in_specs=placed,
        out_specs=(
            P("space", "filt", "chan"),
            P("space", ("chan", "filt"), None),
            P(None, None, None, "filt", "chan"),
        ),
        check_vma=False,
    )
```

time: 351 us -> 62.4 us (0.18)
  waiting for transfers between devices: 228 us -> 0 us
  Pallas kernels: 0 us -> 56.7 us
  local copies, waits for them, and re-layouts: 33.5 us -> 4.27 us
  other arithmetic: 26.6 us -> 0 us
  matrix products: 21.7 us -> 0 us
  between operations: 16 us -> 0.64 us
  starting transfers between devices: 12.9 us -> 0 us
  blocking collectives: 8.42 us -> 0 us
    psum x1 -> x0, waiting for transfers between devices: 228 us -> none  [body(): total = lax.psum(local_grad, 'space')]
    pallas_call x0 -> x1, Pallas kernels: none -> 56.7 us  [body(): pl.pallas_call(functools.partial(kernel, (S, NX, NZ, NY)), out_shape=tupl...]
    dot_general x27 -> x0, matrix products: 21.7 us -> none  [the longest x9 11.5 us: body(): jnp.einsum('zfp,zkp->fk', grad_full, window, preferred_element_type=jnp.f...]
    unnamed x131 -> x3, local copies, waits for them, and re-layouts: 22.2 us -> 4.27 us
    ppermute x4 -> x0, starting transfers between devices: 12.6 us -> none  [the longest x2 6.85 us: padded(): before = lax.ppermute(last, axis, up)]
    mul x5 -> x0, other arithmetic: 11.1 us -> none  [plane_window(): return widened[:, :, begin:begin + plane] * masks[col_step]]
    all_gather x2 -> x0, blocking collectives: 8.42 us -> none  [the longest x1 6.13 us: body(): panels = lax.all_gather(activation, 'filt', axis=1, tiled=True)]
    reshape x1 -> x0, local copies, waits for them, and re-layouts: 8.07 us -> none  [body(): local_grad = jnp.stack(taps).reshape(3, 3, 3, filt_local, chan_local)]
  transfers between devices with their start and end apart: 7 -> 0, of which waited for: 1 -> 0; matrix products, arithmetic and copies ran while one was open for 13% -> 0% of each run, Pallas kernels for 0% -> 0%
where the time goes in v2:
time: 62.4 us; the launch traced here: 61.6 us
  Pallas kernels  56.7 us (91%)
  local copies, waits for them, and re-layouts  4.27 us (7%)
  between operations  0.64 us (1%)
    pallas_call x1, Pallas kernels, body(): pl.pallas_call(functools.partial(kernel, (S, NX, NZ, NY)), out_shape=tupl...  56.7 us
    unnamed x3, local copies, waits for them, and re-layouts  4.27 us

profile of v2, /device:TPU:12, one launch (start us, length us, event | category | flops | bytes accessed | tf_op | source)
XLA Modules:
  0.0 61.6 jit_solution(14135762184114920910)
XLA Ops:
  0.6 56.7 %shard_map.58 = (bf16[1,256,256]{2,1,0:T(8,128)(2,1)S(1)}, bf16[1,128,512]{2,1,0:T(8,128)(2,1)S(1)}, f32[3,3,3,256,256]{4,3,2,1,0:T(8,128)S(1)}) custom-call(bf16[1,128,512]{2,1,0:T(8,128)(2,1)} %act_ref.1, bf16[3,3,3,256,256]{4,3,2,1,0:T(8,128)(2,1)} %w_hbm.1, bf16[1,256,256]{2,1,0:T(8,128)(2,1)} %grad_ref.1), custom_call_target="tpu_custom_call" | custom-call | tf_op jit(solution)/shard_map/pallas_call | solution.py:327
  57.3 0.7 %copy.9 = bf16[1,256,256]{2,1,0:T(8,128)(2,1)} copy(bf16[1,256,256]{2,1,0:T(8,128)(2,1)S(1)} %get-tuple-element.3) | data formatting | bytes 262144
  58.0 0.7 %copy.10 = bf16[1,128,512]{2,1,0:T(8,128)(2,1)} copy(bf16[1,128,512]{2,1,0:T(8,128)(2,1)S(1)} %get-tuple-element.4) | data formatting | bytes 262144
  58.6 3.0 %copy.11 = f32[3,3,3,256,256]{4,3,2,1,0:T(8,128)} copy(f32[3,3,3,256,256]{4,3,2,1,0:T(8,128)S(1)} %get-tuple-element.5) | data formatting | bytes 14155776

commit v3 on v2

--- a/solution.py
+++ b/solution.py
@@ -22,8 +22,8 @@
 
 def kernel(
     sizes, act_ref, w_hbm, grad_ref, out_ref, ig_ref, acc,
-    actg, gradg, wide, gwide, w, facc, bacc, fpart, bpart, frecv, brecv,
-    w_sem, az_send, ay_send, ax_send, gz_send, gy_send, gc_send,
+    actg, gradg, wide, gwide, w, wf, facc, bacc, fpart, bpart, frecv, brecv,
+    w_sem, wf_sem, az_send, ay_send, ax_send, gz_send, gy_send, gc_send,
     a_recv, g_recv, f_send, f_recv, b_send, b_recv,
 ):
     S, NX, NZ, NY = sizes
@@ -135,20 +135,27 @@
     w_copy = pltpu.make_async_copy(w_hbm, w, w_sem)
     w_copy.start()
 
+    def wf_copy(i):
+        a, b, k = i // 9, i // 3 % 3, i % 3
+        return pltpu.make_async_copy(
+            w_hbm.at[a, b, k], wf.at[a, b, :, k * chans : (k + 1) * chans], wf_sem.at[i]
+        )
+
+    for i in range(27):
+        wf_copy(i).start()
+
     for end in (0, S + 1):
         gradg[end] = jnp.zeros((filters, cells), bf16)
         wide[end] = jnp.zeros(wide.shape[1:], bf16)
 
     @pl.loop(1, S + 1)
     def _(j):
-        for k in range(3):
-            wide[j, k, 0:W, :] = jnp.zeros((W, chans), bf16)
-            wide[j, k, W + cells : 2 * W + cells, :] = jnp.zeros((W, chans), bf16)
+        wide[j, 0:W, :] = jnp.zeros((W, 3 * chans), bf16)
+        wide[j, W + cells : 2 * W + cells, :] = jnp.zeros((W, 3 * chans), bf16)
 
     for j in range(3):
-        for k in range(3):
-            gwide[j, k, 0:W, :] = jnp.zeros((W, filters), bf16)
-            gwide[j, k, W + cells : 2 * W + cells, :] = jnp.zeros((W, filters), bf16)
+        gwide[j, 0:W, :] = jnp.zeros((W, gwide.shape[2]), bf16)
+        gwide[j, W + cells : 2 * W + cells, :] = jnp.zeros((W, gwide.shape[2]), bf16)
 
     @pl.loop(0, 27)
     def _(i):
@@ -157,6 +164,10 @@
     facc[...] = jnp.zeros_like(facc)
     bacc[...] = jnp.zeros_like(bacc)
     w_copy.wait()
+    for i in range(27):
+        wf_copy(i).wait()
+
+    lanes = gwide.shape[2] // 3
 
     def b_copy(e):
         to = (x + e) % NX
@@ -169,36 +180,52 @@
         fpart.at[:, pl.ds(pl.multiple_of((1 - c) * half, half), half)], frecv, f_send, f_recv, cpeer
     )
 
+    def window(plane, b):
+        return wide[plane + 1, pl.ds(pl.multiple_of(b * W, W), cells), :]
+
     def backward():
         @pl.loop(0, 3)
         def _(j):
             def store(k, value):
-                gwide[j, k, W : W + cells, :] = value
+                at = (2 - k) * lanes
+                gwide[j, W : W + cells, at : at + filters] = value
 
             shifted_copies(gradg[s + j].astype(f32).T, store)
 
-        @pl.loop(0, 9)
-        def _(i):
-            a, b = i // 3, i % 3
+        @pl.loop(0, 3)
+        def _(a):
             total = None
-            for k in range(3):
-                rows = gwide[2 - a, 2 - k, pl.ds(pl.multiple_of((2 - b) * W, W), cells), :]
-                term = jnp.dot(rows, w[a, b, k], preferred_element_type=f32)
-                total = term if total is None else total + term
+            for b in range(3):
+                rows = slice((2 - b) * W, (2 - b) * W + cells)
+                if lanes == filters:
+                    taps = w[a, b].reshape(3 * filters, chans)
+                    terms = [jnp.dot(gwide[2 - a, rows, :], taps, preferred_element_type=f32)]
+                else:
+                    terms = [
+                        jnp.dot(
+                            gwide[2 - a, rows, k * lanes : k * lanes + filters],
+                            w[a, b, k], preferred_element_type=f32,
+                        )
+                        for k in range(3)
+                    ]
+                for term in terms:
+                    total = term if total is None else total + term
             bacc[...] += total
 
         bpart[...] = bacc[...].T
+
+    def send_backward():
         for e in range(1, NX):
             b_copy(e).start()
 
     def forward():
-        @pl.loop(0, 9)
-        def _(i):
-            a, b = i // 3, i % 3
+        @pl.loop(0, 3)
+        def _(a):
             total = None
-            for k in range(3):
-                rows = wide[s + a, k, pl.ds(pl.multiple_of(b * W, W), cells), :]
-                term = lax.dot_general(rows, w[a, b, k], (((1,), (1,)), ((), ())), preferred_element_type=f32)
+            for b in range(3):
+                term = lax.dot_general(
+                    window(s + a - 1, b), wf[a, b], (((1,), (1,)), ((), ())), preferred_element_type=f32
+                )
                 total = term if total is None else total + term
             facc[...] += total
 
@@ -213,25 +240,41 @@
                 a_wait(plane, (x + e) % NX)
 
             def store(k, value):
-                wide[plane + 1, k, W : W + cells, :] = value
+                wide[plane + 1, W : W + cells, k * chans : (k + 1) * chans] = value
 
             shifted_copies(actg[plane].astype(f32).T, store)
 
     scale = 1.0 / math.sqrt(S * cells)
 
-    def filter_grad(zz):
-        @pl.loop(0, 9)
-        def _(i):
-            b, k = i // 3, i % 3
-            total = None
-            for n in range(NY):
-                j = zz * NY + n
-                rows = wide[j + 1, k, pl.ds(pl.multiple_of(b * W, W), cells), :]
-                grads = gradg[pl.ds(j, 3)].reshape(3 * filters, cells)
-                term = jnp.dot(grads, rows, preferred_element_type=f32)
-                total = term if total is None else total + term
-            for j in range(3):
-                acc[2 - j, b, k] += total[j * filters : (j + 1) * filters] * scale
+    def add(a, b, value):
+        for k in range(3):
+            acc[a, b, k] += value[:, k * chans : (k + 1) * chans] * scale
+
+    def in_pair(zz):
+        @pl.loop(0, 3)
+        def _(b):
+            j = zz * NY
+            grads = gradg[pl.ds(j + 1, 2)].reshape(2 * filters, cells)
+            low = jnp.dot(grads, window(j, b), preferred_element_type=f32)
+            high = jnp.dot(grads, window(j + 1, b), preferred_element_type=f32)
+            add(0, b, low[filters:])
+            add(1, b, low[:filters] + high[filters:])
+            add(2, b, high[:filters])
+
+    def across_pairs(zz):
+        @pl.loop(0, 3)
+        def _(b):
+            j = zz * NY + 1
+            add(0, b, jnp.dot(gradg[j + 2], window(j, b), preferred_element_type=f32))
+            add(2, b, jnp.dot(gradg[j + 1], window(j + 1, b), preferred_element_type=f32))
+
+    def filter_grad(zz, way):
+        prepare(zz)
+        in_pair(zz)
+
+        @pl.when(zz != z)
+        def _():
+            across_pairs(zz + (-1 - way) // 2)
 
     def relay(zz, way, wait, along, across, last):
         plane = zz * NY + y
@@ -274,17 +317,14 @@
         def _():
             backward()
 
-        @pl.when(d >= 2)
-        def _():
-            at_distance(d - 2, lambda zz, way: prepare(zz))
-
-        @pl.when(d == 3)
-        def _():
+        @pl.when(d == 4)
+        def _():
+            send_backward()
             forward()
 
-        @pl.when(d >= 2)
-        def _():
-            at_distance(d - 2, lambda zz, way: filter_grad(zz))
+        @pl.when(d != 2)
+        def _():
+            at_distance(jnp.maximum(d - 2, 0), filter_grad)
 
     f_copy.wait()
     out_ref[0] = (fpart[:, pl.ds(pl.multiple_of(c * half, half), half)] + frecv[...]).astype(bf16)
@@ -332,16 +372,17 @@
         scratch_shapes=[
             pltpu.VMEM((S, chans, cells), bf16),
             pltpu.VMEM((S + 2, filters, cells), bf16),
-            pltpu.VMEM((S + 2, 3, cells + 2 * W, chans), bf16),
-            pltpu.VMEM((3, 3, cells + 2 * W, filters), bf16),
+            pltpu.VMEM((S + 2, cells + 2 * W, 3 * chans), bf16),
+            pltpu.VMEM((3, cells + 2 * W, 3 * pl.cdiv(filters, 128) * 128), bf16),
             pltpu.VMEM(weights.shape, bf16),
+            pltpu.VMEM((3, 3, filters, 3 * chans), bf16),
             pltpu.VMEM((cells, filters), f32),
             pltpu.VMEM((cells, chans), f32),
             pltpu.VMEM((filters, cells), f32),
             pltpu.VMEM((chans, cells), f32),
             pltpu.VMEM((filters, half), f32),
             pltpu.VMEM((NX - 1, cb, cells), f32),
-            dma,
+            dma, dma((27,)),
             dma((2 * NZ,)), dma((NZ,)), dma((S * (NX - 1),)),
             dma((2 * NZ,)), dma((NZ,)), dma((S,)),
             dma((S * NX,)), dma((S * 2,)),

time: 62.4 us -> 54 us (0.87)
  the two profiles are of different devices: /device:TPU:12 before, /device:TPU:1 now
where the time goes in v3:
time: 54 us; the launch traced here: 53.9 us
  Pallas kernels  49 us (91%)
  local copies, waits for them, and re-layouts  4.27 us (8%)
  between operations  0.64 us (1%)
    pallas_call x1, Pallas kernels, body(): pl.pallas_call(functools.partial(kernel, (S, NX, NZ, NY)), out_shape=tupl...  49 us
    unnamed x3, local copies, waits for them, and re-layouts  4.27 us

profile of v3, /device:TPU:1, one launch (start us, length us, event | category | flops | bytes accessed | tf_op | source)
XLA Modules:
  0.0 53.9 jit_solution(10705752182246274318)
XLA Ops:
  0.6 49.0 %shard_map.58 = (bf16[1,256,256]{2,1,0:T(8,128)(2,1)S(1)}, bf16[1,128,512]{2,1,0:T(8,128)(2,1)S(1)}, f32[3,3,3,256,256]{4,3,2,1,0:T(8,128)S(1)}) custom-call(bf16[1,128,512]{2,1,0:T(8,128)(2,1)} %act_ref.1, bf16[3,3,3,256,256]{4,3,2,1,0:T(8,128)(2,1)} %w_hbm.1, bf16[1,256,256]{2,1,0:T(8,128)(2,1)} %grad_ref.1), custom_call_target="tpu_custom_call" | custom-call | tf_op jit(solution)/shard_map/pallas_call | solution.py:367
  49.6 0.7 %copy.9 = bf16[1,256,256]{2,1,0:T(8,128)(2,1)} copy(bf16[1,256,256]{2,1,0:T(8,128)(2,1)S(1)} %get-tuple-element.3) | data formatting | bytes 262144
  50.3 0.7 %copy.10 = bf16[1,128,512]{2,1,0:T(8,128)(2,1)} copy(bf16[1,128,512]{2,1,0:T(8,128)(2,1)S(1)} %get-tuple-element.4) | data formatting | bytes 262144
  50.9 3.0 %copy.11 = f32[3,3,3,256,256]{4,3,2,1,0:T(8,128)} copy(f32[3,3,3,256,256]{4,3,2,1,0:T(8,128)S(1)} %get-tuple-element.5) | data formatting | bytes 14155776
